TPU v7x, 512 devices: a whole 4x8x8 slice. The times are simulated.
512 devices in a mesh: tm: 32 (over y, z_lo), row: 16 (over x, z_hi, core).
Axes of the slice: x: 4, y: 8, z: 8 (z_hi: 2, z_lo: 4; z = z_hi * 4 + z_lo), core: 2. Of those that a mesh axis runs over, the one named last changes fastest.
Arguments:
- latents: bfloat16 [64, 96, 80, 256], P('tm', 'row'), may hold values from -6 to 6
- conv_weight: bfloat16 [3, 3, 768, 256], replicated, may hold values from -0.078125 to 0.078125
- norm_gain: float32 [256], replicated, may hold values from 0.1 to 1.9
- depth_target: bfloat16 [64, 96, 80, 128], P('tm', 'row'), may hold values from -6 to 6
Outputs:
- features: bfloat16 [64, 96, 80, 256], P('tm', 'row')
- gram: float32 [256, 256], replicated
- cross: float32 [256, 128], replicated
All inputs are finite; a program needn't handle non-finite values.
Results may differ from a plain program's by a relative error of at most 0.003.
Values may be sent and summed in bfloat16 or wider, within the bound.
A program may use at most 64 MiB of HBM per device.

v0:
```python
import jax
import jax.numpy as jnp
from jax import lax
from jax.sharding import PartitionSpec as P


def from_behind(value, axis, steps):
    count = lax.axis_size(axis)
    first, last = (max(0, -steps), min(count, count - steps))
    return lax.ppermute(value, axis, [(source, source + steps) for source in range(first, last)])


def extended(cells, sides, width):
    for axis, dim in sides:
        count = lax.axis_size(axis)
        ends = count - 1
        head = lax.slice_in_dim(cells, 0, width, axis=dim)
        tail = lax.slice_in_dim(cells, cells.shape[dim] - width, cells.shape[dim], axis=dim)
        cells = jnp.concatenate(
            [
                lax.ppermute(tail, axis, [(i, (i + 1) % count) for i in range(ends)]),
                cells,
                lax.ppermute(head, axis, [((i + 1) % count, i) for i in range(ends)]),
            ],
            axis=dim,
        )
    return cells


def convolve(padded, conv_weight):
    frames = padded.shape[0] - 2
    rows = padded.shape[1] - 2
    cols = padded.shape[2]
    chans = conv_weight.shape[3]
    wide = jnp.pad(padded, ((0, 0), (0, 0), (1, 1), (0, 0)))
    stacked = jnp.concatenate(
        [wide[:, :, 0:cols], wide[:, :, 1 : cols + 1], wide[:, :, 2 : cols + 2]], axis=3
    )
    total = jnp.zeros((frames * rows * cols, chans), jnp.float32)
    for dtime in range(3):
        for drow in range(3):
            piece = stacked[dtime : dtime + frames, drow : drow + rows].reshape(
                frames * rows * cols, -1
            )
            total = total + jnp.dot(
                piece, conv_weight[dtime, drow], preferred_element_type=jnp.float32
            )
    return total


def on_device(latents, conv_weight, norm_gain, depth_target):
    cached = from_behind(latents, "tm", 1)
    joined = jnp.concatenate([cached, latents], axis=0)
    padded = extended(joined, (("row", 1),), 1)
    conv = convolve(padded, conv_weight)
    flat_in = latents.reshape(conv.shape[0], conv.shape[1]).astype(jnp.float32)
    normed = conv * jax.lax.rsqrt(jnp.mean(conv * conv, axis=1, keepdims=True) + 1e-06) * norm_gain
    flat = (flat_in + jax.nn.silu(normed)).astype(jnp.bfloat16)
    targets = depth_target.reshape(flat.shape[0], -1)
    gram_part = jnp.dot(flat.T, flat, preferred_element_type=jnp.float32)
    cross_part = jnp.dot(flat.T, targets, preferred_element_type=jnp.float32)
    count = flat.shape[0] * lax.axis_size("tm") * lax.axis_size("row")
    gram_sum, cross_sum = lax.psum((gram_part, cross_part), ("tm", "row"))
    return (flat.reshape(latents.shape), gram_sum / count, cross_sum / count)


def solution(mesh):
    in_specs = (P("tm", "row", None, None), P(), P(), P("tm", "row", None, None))
    out_specs = (P("tm", "row", None, None), P(), P())
    return jax.shard_map(
        on_device, mesh=mesh, in_specs=in_specs, out_specs=out_specs, check_vma=False
    )
```

profile of v0, /device:TPU:1, one launch (start us, length us, event | category | flops | bytes accessed | tf_op | source)
XLA Modules:
  0.0 338.9 jit_solution(941491397047165075)
XLA Ops:
  7.2 0.0 copy-start
  7.2 0.0 all-reduce.4.cloned.1.call-start
  7.2 5.0 %collective-permute-start = (bf16[2,6,80,256]{3,2,1,0:T(8,128)(2,1)}, bf16[2,6,80,256]{3,2,1,0:T(8,128)(2,1)S(1)}, u32[]{:S(2)}, u32[]{:S(2)}) collective-permute-start(bf16[2,6,80,256]{3,2,1,0:T(8,128)(2,1)} %param.4), channel_id=1, source_target_pairs={{0,16},{16,32},{32,48},{48,64},{64,80},{80,96},{96,112},{112,128},... | collective-permute-start | bytes 1474568 | tf_op jit(solution)/shard_map/ppermute | solution.py:10
  12.2 7.8 %collective-permute-done = bf16[2,6,80,256]{3,2,1,0:T(8,128)(2,1)S(1)} collective-permute-done((bf16[2,6,80,256]{3,2,1,0:T(8,128)(2,1)}, bf16[2,6,80,256]{3,2,1,0:T(8,128)(2,1)S(1)}, u32[]{:S(2)}, u32[]{:S(2)}) %collective-permute-start) | collective-permute-done | bytes 491552 | tf_op jit(solution)/shard_map/ppermute | solution.py:10
  20.1 1.1 constant_dynamic-update-slice_fusion
  21.2 13.5 %collective-permute-start.1 = (bf16[4,1,80,256]{3,2,1,0:T(8,128)(2,1)S(1)}, bf16[4,1,80,256]{3,2,1,0:T(8,128)(2,1)S(1)}, u32[]{:S(2)}, u32[]{:S(2)}) collective-permute-start(bf16[4,1,80,256]{3,2,1,0:T(8,128)(2,1)S(1)} %get-tuple-element.16), channel_id=1, source_target_pairs={{0,1},{1,2},{2,3},{3,4},{4,5},{5,6},{6,7},{7,8},{8,9},{9,10},{10,1... | collective-permute-start | bytes 491528 | tf_op jit(solution)/shard_map/ppermute | solution.py:21
  34.7 1.9 collective-permute-start.2
  36.6 2.1 collective-permute-done.1
  38.7 7.3 %collective-permute-done.2 = bf16[4,1,80,256]{3,2,1,0:T(8,128)(2,1)S(1)} collective-permute-done((bf16[4,1,80,256]{3,2,1,0:T(8,128)(2,1)S(1)}, bf16[4,1,80,256]{3,2,1,0:T(8,128)(2,1)S(1)}, u32[]{:S(2)}, u32[]{:S(2)}) %collective-permute-start.2) | collective-permute-done | bytes 163872 | tf_op jit(solution)/shard_map/ppermute | solution.py:23
  46.0 0.8 fusion.5
  46.7 0.9 fusion.41
  47.6 0.3 pad_maximum_fusion
  48.0 0.0 copy-start.1
  48.0 1.2 fusion.40
  49.2 0.7 copy-done.1
  50.0 0.5 fusion.14
  50.5 0.5 fusion.16
  51.1 0.5 fusion.18
  51.6 0.5 fusion.20
  52.2 0.5 fusion.22
  52.8 0.5 fusion.24
  53.3 0.5 fusion.26
  53.9 0.5 fusion.28
  54.4 0.0 copy-start.2
  54.4 0.0 copy-start.4
  54.5 0.9 multiply_reduce_fusion
  55.4 0.1 copy-done.2
  55.5 0.0 copy-done.4
  55.5 0.4 fusion.13
  55.9 0.0 copy-start.3
  55.9 1.1 fusion.43
  56.9 0.0 copy-done
  56.9 1.0 fusion.44
  57.9 0.0 all-reduce.4.cloned.1.call-update
  58.0 270.9 %all-reduce.4.cloned.1.call-done = (f32[256,256]{1,0:T(8,128)}, f32[256,128]{1,0:T(8,128)}) async-done(((f32[256,256]{1,0:T(8,128)}, f32[256,128]{1,0:T(8,128)}), (f32[256,256]{1,0:T(8,128)}, f32[256,128]{1,0:T(8,128)})) %all-reduce.4.cloned.1.call-update) | async-done | bytes 393232 | tf_op jit(solution)/shard_map/psum | solution.py:63
  328.8 1.7 broadcast_multiply_fusion
  330.5 0.0 copy-done.3
  330.5 1.6 broadcast_multiply_fusion.1
  (3 shorter events, 0.1 us)
Async XLA Ops:
  7.2 49.8 %copy-start = (bf16[2,6,80,128]{3,2,1,0:T(8,128)(2,1)S(1)}, bf16[2,6,80,128]{3,2,1,0:T(8,128)(2,1)}, u32[]{:S(2)}) copy-start(bf16[2,6,80,128]{3,2,1,0:T(8,128)(2,1)} %param.7) | copy-start | bytes 737284
  7.2 321.6 %all-reduce.4.cloned.1.call-start = ((), (), s32[]{:S(2)}) async-start(), calls=%async_computation | async-start | bytes 786432 | tf_op jit(solution)/shard_map/psum | solution.py:63
  7.2 12.8 %collective-permute-start = (bf16[2,6,80,256]{3,2,1,0:T(8,128)(2,1)}, bf16[2,6,80,256]{3,2,1,0:T(8,128)(2,1)S(1)}, u32[]{:S(2)}, u32[]{:S(2)}) collective-permute-start(bf16[2,6,80,256]{3,2,1,0:T(8,128)(2,1)} %param.4), channel_id=1, source_target_pairs={{0,16},{16,32},{32,48},{48,64},{64,80},{80,96},{96,112},{112,128},... | collective-permute-start | bytes 1474568 | tf_op jit(solution)/shard_map/ppermute | solution.py:10
  21.2 17.5 %collective-permute-start.1 = (bf16[4,1,80,256]{3,2,1,0:T(8,128)(2,1)S(1)}, bf16[4,1,80,256]{3,2,1,0:T(8,128)(2,1)S(1)}, u32[]{:S(2)}, u32[]{:S(2)}) collective-permute-start(bf16[4,1,80,256]{3,2,1,0:T(8,128)(2,1)S(1)} %get-tuple-element.16), channel_id=1, source_target_pairs={{0,1},{1,2},{2,3},{3,4},{4,5},{5,6},{6,7},{7,8},{8,9},{9,10},{10,1... | collective-permute-start | bytes 491528 | tf_op jit(solution)/shard_map/ppermute | solution.py:21
  34.7 11.3 %collective-permute-start.2 = (bf16[4,1,80,256]{3,2,1,0:T(8,128)(2,1)S(1)}, bf16[4,1,80,256]{3,2,1,0:T(8,128)(2,1)S(1)}, u32[]{:S(2)}, u32[]{:S(2)}) collective-permute-start(bf16[4,1,80,256]{3,2,1,0:T(8,128)(2,1)S(1)} %get-tuple-element.17), channel_id=1, source_target_pairs={{1,0},{2,1},{3,2},{4,3},{5,4},{6,5},{7,6},{8,7},{9,8},{10,9},{11,1... | collective-permute-start | bytes 491528 | tf_op jit(solution)/shard_map/ppermute | solution.py:23
  48.0 2.0 copy-start.1
  54.4 1.0 copy-start.2
  54.4 1.0 copy-start.4
  55.9 274.6 %copy-start.3 = (bf16[960,256]{1,0:T(8,128)(2,1)}, bf16[960,256]{1,0:T(8,128)(2,1)S(1)}, u32[]{:S(2)}) copy-start(bf16[960,256]{1,0:T(8,128)(2,1)S(1)} %fusion.13) | copy-start | bytes 1474564
Sparse Core Ops, SparseCore 0:
  58.1 270.6 all-reduce.3
where the time goes:
time: 339 us
  waiting for transfers between devices  288 us (85%)
  starting transfers between devices  20.4 us (6%)
  between operations  14.2 us (4%)
  matrix products  7.34 us (2%)
  other arithmetic  4.74 us (1%)
  local copies, waits for them, and re-layouts  4.12 us (1%)
    psum x1, waiting for transfers between devices, on_device(): gram_sum, cross_sum = lax.psum((gram_part, cross_part), ('tm', 'row'))  271 us
    ppermute x1, starting transfers between devices, extended(): lax.ppermute(tail, axis, [(i, (i + 1) % count) for i in range(ends)])  13.5 us
    ppermute x1, waiting for transfers between devices, from_behind(): lax.ppermute(value, axis, [(source, source + steps) for source in range(f...  7.81 us
    ppermute x1, waiting for transfers between devices, extended(): lax.ppermute(head, axis, [((i + 1) % count, i) for i in range(ends)])  7.3 us
  transfers between devices with their start and end apart: 4, of which 4 were waited for; matrix products, arithmetic and copies ran while one was open for 0% of the time, Pallas kernels for 0%

commit v1 on v0

--- a/solution.py
+++ b/solution.py
@@ -60,7 +60,11 @@
     gram_part = jnp.dot(flat.T, flat, preferred_element_type=jnp.float32)
     cross_part = jnp.dot(flat.T, targets, preferred_element_type=jnp.float32)
     count = flat.shape[0] * lax.axis_size("tm") * lax.axis_size("row")
-    gram_sum, cross_sum = lax.psum((gram_part, cross_part), ("tm", "row"))
+
+    def measure_streams(x_local):
+        return lax.psum(lax.psum(x_local, "tm"), "row")
+
+    gram_sum, cross_sum = measure_streams((gram_part, cross_part))
     return (flat.reshape(latents.shape), gram_sum / count, cross_sum / count)
 
 

time: 339 us -> 556 us (1.64)
  waiting for transfers between devices: 288 us -> 505 us
    psum x1 -> x2, waiting for transfers between devices: 271 us -> 488 us  [measure_streams(): return lax.psum(lax.psum(x_local, 'tm'), 'row')]
  transfers between devices with their start and end apart: 4 -> 5, of which waited for: 4 -> 5; matrix products, arithmetic and copies ran while one was open for 0% -> 0% of each run, Pallas kernels for 0% -> 0%
where the time goes in v1:
time: 556 us
  waiting for transfers between devices  505 us (91%)
  starting transfers between devices  20.5 us (4%)
  between operations  14.2 us (3%)
  matrix products  7.34 us (1%)
    psum x2, waiting for transfers between devices, measure_streams(): return lax.psum(lax.psum(x_local, 'tm'), 'row')  488 us
    ppermute x1, starting transfers between devices, extended(): lax.ppermute(tail, axis, [(i, (i + 1) % count) for i in range(ends)])  13.5 us
  transfers between devices with their start and end apart: 5, of which 5 were waited for; matrix products, arithmetic and copies ran while one was open for 0% of the time, Pallas kernels for 0%

profile of v1, /device:TPU:1, one launch (start us, length us, event | category | flops | bytes accessed | tf_op | source)
XLA Modules:
  0.0 555.8 jit_solution(18262894178746923875)
XLA Ops:
  7.2 0.0 copy-start
  7.2 0.0 all-reduce.6.cloned.1.call-start
  7.2 5.0 collective-permute-start
  12.2 7.8 %collective-permute-done = bf16[2,6,80,256]{3,2,1,0:T(8,128)(2,1)S(1)} collective-permute-done((bf16[2,6,80,256]{3,2,1,0:T(8,128)(2,1)}, bf16[2,6,80,256]{3,2,1,0:T(8,128)(2,1)S(1)}, u32[]{:S(2)}, u32[]{:S(2)}) %collective-permute-start) | collective-permute-done | bytes 491552 | tf_op jit(solution)/shard_map/ppermute | solution.py:10
  20.1 1.1 constant_dynamic-update-slice_fusion
  21.2 13.5 %collective-permute-start.1 = (bf16[4,1,80,256]{3,2,1,0:T(8,128)(2,1)S(1)}, bf16[4,1,80,256]{3,2,1,0:T(8,128)(2,1)S(1)}, u32[]{:S(2)}, u32[]{:S(2)}) collective-permute-start(bf16[4,1,80,256]{3,2,1,0:T(8,128)(2,1)S(1)} %get-tuple-element.18), channel_id=1, source_target_pairs={{0,1},{1,2},{2,3},{3,4},{4,5},{5,6},{6,7},{7,8},{8,9},{9,10},{10,1... | collective-permute-start | bytes 491528 | tf_op jit(solution)/shard_map/ppermute | solution.py:21
  34.7 1.9 collective-permute-start.2
  36.6 2.1 collective-permute-done.1
  38.7 7.3 %collective-permute-done.2 = bf16[4,1,80,256]{3,2,1,0:T(8,128)(2,1)S(1)} collective-permute-done((bf16[4,1,80,256]{3,2,1,0:T(8,128)(2,1)S(1)}, bf16[4,1,80,256]{3,2,1,0:T(8,128)(2,1)S(1)}, u32[]{:S(2)}, u32[]{:S(2)}) %collective-permute-start.2) | collective-permute-done | bytes 163872 | tf_op jit(solution)/shard_map/ppermute | solution.py:23
  46.0 0.8 fusion.5
  46.7 0.9 fusion.41
  47.6 0.3 pad_maximum_fusion
  48.0 0.0 copy-start.1
  48.0 1.2 fusion.40
  49.2 0.7 copy-done.1
  50.0 0.5 fusion.14
  50.5 0.5 fusion.16
  51.1 0.5 fusion.18
  51.6 0.5 fusion.20
  52.2 0.5 fusion.22
  52.8 0.5 fusion.24
  53.3 0.5 fusion.26
  53.9 0.5 fusion.28
  54.4 0.0 copy-start.2
  54.4 0.0 copy-start.4
  54.5 0.9 multiply_reduce_fusion
  55.4 0.1 copy-done.2
  55.5 0.0 copy-done.4
  55.5 0.4 fusion.13
  55.9 0.0 copy-start.3
  55.9 1.1 fusion.43
  56.9 0.0 copy-done
  56.9 1.0 fusion.44
  57.9 0.0 all-reduce.6.cloned.1.call-update
  58.0 0.0 all-reduce.8.cloned.1.call-start
  58.0 280.6 %all-reduce.6.cloned.1.call-done = (f32[256,256]{1,0:T(8,128)}, f32[256,128]{1,0:T(8,128)}) async-done(((f32[256,256]{1,0:T(8,128)}, f32[256,128]{1,0:T(8,128)}), (f32[256,256]{1,0:T(8,128)}, f32[256,128]{1,0:T(8,128)})) %all-reduce.6.cloned.1.call-update) | async-done | bytes 393232 | tf_op jit(solution)/shard_map/psum | solution.py:65
  338.6 0.0 all-reduce.8.cloned.1.call-update
  338.6 207.1 %all-reduce.8.cloned.1.call-done = (f32[256,256]{1,0:T(8,128)}, f32[256,128]{1,0:T(8,128)}) async-done(((f32[256,256]{1,0:T(8,128)}, f32[256,128]{1,0:T(8,128)}), (f32[256,256]{1,0:T(8,128)}, f32[256,128]{1,0:T(8,128)})) %all-reduce.8.cloned.1.call-update) | async-done | bytes 393232 | tf_op jit(solution)/shard_map/psum | solution.py:65
  545.7 1.7 broadcast_multiply_fusion
  547.4 0.0 copy-done.3
  547.4 1.6 broadcast_multiply_fusion.1
  (3 shorter events, 0.1 us)
Async XLA Ops:
  7.2 49.8 %copy-start = (bf16[2,6,80,128]{3,2,1,0:T(8,128)(2,1)S(1)}, bf16[2,6,80,128]{3,2,1,0:T(8,128)(2,1)}, u32[]{:S(2)}) copy-start(bf16[2,6,80,128]{3,2,1,0:T(8,128)(2,1)} %param.7) | copy-start | bytes 737284
  7.2 331.4 %all-reduce.6.cloned.1.call-start = ((), (), s32[]{:S(2)}) async-start(), calls=%async_computation | async-start | bytes 786432 | tf_op jit(solution)/shard_map/psum | solution.py:65
  7.2 12.8 %collective-permute-start = (bf16[2,6,80,256]{3,2,1,0:T(8,128)(2,1)}, bf16[2,6,80,256]{3,2,1,0:T(8,128)(2,1)S(1)}, u32[]{:S(2)}, u32[]{:S(2)}) collective-permute-start(bf16[2,6,80,256]{3,2,1,0:T(8,128)(2,1)} %param.4), channel_id=1, source_target_pairs={{0,16},{16,32},{32,48},{48,64},{64,80},{80,96},{96,112},{112,128},... | collective-permute-start | bytes 1474568 | tf_op jit(solution)/shard_map/ppermute | solution.py:10
  21.2 17.5 %collective-permute-start.1 = (bf16[4,1,80,256]{3,2,1,0:T(8,128)(2,1)S(1)}, bf16[4,1,80,256]{3,2,1,0:T(8,128)(2,1)S(1)}, u32[]{:S(2)}, u32[]{:S(2)}) collective-permute-start(bf16[4,1,80,256]{3,2,1,0:T(8,128)(2,1)S(1)} %get-tuple-element.18), channel_id=1, source_target_pairs={{0,1},{1,2},{2,3},{3,4},{4,5},{5,6},{6,7},{7,8},{8,9},{9,10},{10,1... | collective-permute-start | bytes 491528 | tf_op jit(solution)/shard_map/ppermute | solution.py:21
  34.7 11.3 %collective-permute-start.2 = (bf16[4,1,80,256]{3,2,1,0:T(8,128)(2,1)S(1)}, bf16[4,1,80,256]{3,2,1,0:T(8,128)(2,1)S(1)}, u32[]{:S(2)}, u32[]{:S(2)}) collective-permute-start(bf16[4,1,80,256]{3,2,1,0:T(8,128)(2,1)S(1)} %get-tuple-element.19), channel_id=1, source_target_pairs={{1,0},{2,1},{3,2},{4,3},{5,4},{6,5},{7,6},{8,7},{9,8},{10,9},{11,1... | collective-permute-start | bytes 491528 | tf_op jit(solution)/shard_map/ppermute | solution.py:23
  48.0 2.0 copy-start.1
  54.4 1.0 copy-start.2
  54.4 1.0 copy-start.4
  55.9 491.5 %copy-start.3 = (bf16[960,256]{1,0:T(8,128)(2,1)}, bf16[960,256]{1,0:T(8,128)(2,1)S(1)}, u32[]{:S(2)}) copy-start(bf16[960,256]{1,0:T(8,128)(2,1)S(1)} %fusion.13) | copy-start | bytes 1474564
  58.0 487.8 %all-reduce.8.cloned.1.call-start = ((), (), s32[]{:S(2)}) async-start(), calls=%async_computation.1 | async-start | bytes 786432 | tf_op jit(solution)/shard_map/psum | solution.py:65
Sparse Core Ops, SparseCore 0:
  58.1 280.4 all-reduce.5
  341.5 204.1 all-reduce.7
